TPU v7x, 32 devices: a whole 2x2x4 slice. The times are simulated.
32 devices in a mesh: band: 16 (over z, y, core), grid: 2 (over x).
Axes of the slice: x: 2, y: 2, z: 4, core: 2. Of those that a mesh axis runs over, the one named last changes fastest.
Arguments:
- orbitals: float32 [32, 48, 2304], P('band', 'grid'), may hold values from -6 to 6
- occupation: float32 [32], P('band'), may hold values from 0.2 to 1
Outputs:
- exchange: float32 [32, 48, 2304], P('band', 'grid')
All inputs are finite; a program needn't handle non-finite values.
Results may differ from a plain program's by a relative error of at most 0.0003.
Values sent between devices are 32-bit elements; how exact they have to be, the bound alone decides.
A program may use at most 64 MiB of HBM per device.

v0:
```python
import jax
import jax.numpy as jnp
import numpy as np
from jax import lax
from jax.experimental import pallas as pl
from jax.experimental.pallas import tpu as pltpu
from jax.sharding import PartitionSpec as P

N = 48
HALF = N // 2
PLANE = N * N
COLS = PLANE // 2
STOPS = 3
CUTS = [(0, 256), (256, 256), (512, 256), (768, 256), (1024, 128)]


def cas(product, length):
    angle = (product % length) * (2.0 * np.pi / length)
    return np.cos(angle) + np.sin(angle)


def tables():
    i, h = np.arange(N), np.arange(HALF)
    along_z = np.tile(cas(i[:, None] * i[None, :], N), (1, HALF))
    even = cas(2 * h[:, None] * h[None, :], N)
    odd = cas(h[:, None] * (2 * h[None, :] + 1), N)
    along_y = np.stack([np.repeat(m, N, axis=1) for m in (even, odd, odd.T)])
    along_x = cas(i[:, None] * i[None, :], N)
    square = np.where(i <= HALF, i, i - N).astype(np.float64) ** 2
    order = np.concatenate([i[0::2], i[1::2]])
    total = square[:, None, None] + square[order][None, :, None] + square[None, None, :]
    coulomb = np.where(total > 0, 24.0 * 24.0 / np.pi / np.where(total > 0, total, 1.0), 0.0)
    coulomb = coulomb.reshape(N, PLANE) * (-0.25 / N**3)
    x_high = along_x.astype(np.float32).astype(jnp.bfloat16)
    x_low = (along_x - x_high.astype(np.float64)).astype(np.float32).astype(jnp.bfloat16)
    along_x = np.concatenate([x_high, x_high, x_low], axis=1)
    return (
        along_z.astype(np.float32),
        along_y.astype(np.float32),
        along_x,
        coulomb.astype(np.float32),
    )


def split(value):
    high = value.astype(jnp.bfloat16)
    return high, (value - high.astype(jnp.float32)).astype(jnp.bfloat16)


def dot(a, b):
    return jnp.dot(a, b, preferred_element_type=jnp.float32)


def build(along_z, along_y, w_high, w_low):
    for m in range(3):

        @pl.loop(0, HALF)
        def _(y):
            rows = pl.ds(pl.multiple_of(y * N, 16), N)
            high, low = split(along_z[...] * along_y[m, pl.ds(y, 1), :])
            w_high[m, rows, :] = high
            w_low[m, rows, :] = low


def pairs(mine, visits, acc, along_x, coulomb, w_high, w_low, lhs, xrhs):
    for p in range(2):
        hi, lo = slice(p * N, (p + 1) * N), slice((p + 2) * N, (p + 3) * N)
        for start in range(0, COLS, 128):
            left, right = slice(start, start + 128), slice(COLS + start, COLS + start + 128)
            first = mine(left) * visits(p, left)
            second = mine(right) * visits(p, right)
            for parity, value in enumerate((first + second, first - second)):
                lhs[parity, hi, left], lhs[parity, lo, left] = split(value)

    def yz(which, parity, cut):
        both = dot(lhs[parity], w_high[which, :, cut])
        return both[: 2 * N] + both[2 * N :] + dot(lhs[parity, : 2 * N, :], w_low[which, :, cut])

    for parity in range(2):
        for start, size in CUTS:
            value = yz(parity, parity, slice(start, start + size))
            high, low = split(value)
            to = slice(parity * COLS + start, parity * COLS + start + size)
            for p in range(2):
                rows = slice(p * N, (p + 1) * N)
                xrhs[p, :N, to] = high[rows]
                xrhs[p, N : 2 * N, to] = low[rows]
                xrhs[p, 2 * N :, to] = high[rows]
    for parity in range(2):
        for start, size in CUTS:
            at = slice(parity * COLS + start, parity * COLS + start + size)
            for p in range(2):
                work = dot(along_x[...], xrhs[p, :, at]) * coulomb[:, at]
                high, low = split(work)
                work = dot(along_x[...], jnp.concatenate([high, low, high], axis=0))
                high, low = split(work)
                lhs[parity, p * N : (p + 1) * N, start : start + size] = high
                lhs[parity, (p + 2) * N : (p + 3) * N, start : start + size] = low
    for start, size in CUTS:
        left, right = slice(start, start + size), slice(COLS + start, COLS + start + size)
        even, odd = yz(0, 0, left), yz(2, 1, left)
        for at, value in ((left, even + odd), (right, even - odd)):
            acc[:, at] += value[:N] * visits(0, at) + value[N:] * visits(1, at)


def kernel(mine_ref, visit_ref, along_z, along_y, along_x, coulomb, out, w_high, w_low, lhs, xrhs):
    build(along_z, along_y, w_high, w_low)
    out[...] = jnp.zeros_like(out)

    @pl.loop(0, STOPS)
    def _(stop):
        pairs(
            lambda at: mine_ref[:, at],
            lambda p, at: visit_ref[stop * 2 + p, :, at],
            out, along_x, coulomb, w_high, w_low, lhs, xrhs,
        )


def per_device(orbitals, occupation):
    count, slab, plane = orbitals.shape
    root = jnp.sqrt(occupation)
    devices = lax.axis_size("band")
    place = lax.axis_index("grid")
    route = [((i + 1) % devices, i) for i in range(devices)]
    block = lax.all_gather(orbitals * root[:, None, None], "grid", axis=1, tiled=True)
    blocks = [block]
    for _ in range(1, STOPS):
        blocks.append(lax.ppermute(blocks[-1], "band", route))
    mine = lax.dynamic_index_in_dim(block, place, 0, keepdims=False)
    scale = 1.0 / lax.dynamic_index_in_dim(root, place, 0, keepdims=False)
    vmem = pl.BlockSpec(memory_space=pltpu.VMEM)
    result = pl.pallas_call(
        kernel,
        out_shape=jax.ShapeDtypeStruct((N, plane), jnp.float32),
        in_specs=[vmem] * 6,
        out_specs=vmem,
        scratch_shapes=[
            pltpu.VMEM((3, COLS, COLS), jnp.bfloat16),
            pltpu.VMEM((3, COLS, COLS), jnp.bfloat16),
            pltpu.VMEM((2, 4 * N, COLS), jnp.bfloat16),
            pltpu.VMEM((2, 3 * N, PLANE), jnp.bfloat16),
        ],
        compiler_params=pltpu.CompilerParams(vmem_limit_bytes=50 << 20),
    )(mine, jnp.concatenate(blocks), *[jnp.asarray(t) for t in tables()])
    result = (result * scale).reshape(2, 1, slab, plane)
    result = lax.all_to_all(result, "grid", 0, 1)
    return result.reshape(count, slab, plane)


def solution(mesh):
    placed = (P("band", "grid", None), P("band"))
    return jax.shard_map(
        per_device, mesh=mesh, in_specs=placed, out_specs=P("band", "grid", None), check_vma=False
    )
```

profile of v0, /device:TPU:0, one launch (start us, length us, event | category | flops | bytes accessed | tf_op | source)
XLA Modules:
  0.0 75.4 jit_solution(3511425122485174779)
XLA Ops:
  0.0 0.7 sqrt.3
  0.7 1.1 %broadcast_multiply_fusion.1 = f32[2,24,2304]{2,1,0:T(8,128)S(1)} fusion(f32[2,24,2304]{2,1,0:T(8,128)} %param.6, f32[2]{0:T(128)S(1)} %sqrt.3), kind=kLoop, calls=%fused_computation.3 | loop fusion | flops 110592 | bytes 884744 | tf_op jit(solution)/shard_map/mul | solution.py:125
  1.8 13.8 %all_gather.3 = f32[2,48,2304]{2,1,0:T(8,128)S(1)} all-gather(f32[2,24,2304]{2,1,0:T(8,128)S(1)} %broadcast_multiply_fusion.1), channel_id=1, replica_groups=mesh['band'=16,'grid'=2] {'grid'}, dimensions={1}, use_global_device_ids=true | all-gather | bytes 1327104 | tf_op jit(solution)/shard_map/all_gather | solution.py:125
  15.6 3.4 %collective-permute-start = (f32[2,48,2304]{2,1,0:T(8,128)S(1)}, f32[2,48,2304]{2,1,0:T(8,128)S(1)}, u32[]{:S(2)}, u32[]{:S(2)}) collective-permute-start(f32[2,48,2304]{2,1,0:T(8,128)S(1)} %all_gather.3), channel_id=1, source_target_pairs={{2,0},{4,2},{6,4},{8,6},{10,8},{12,10},{14,12},{16,14},{18,16},{20... | collective-permute-start | bytes 2654216 | tf_op jit(solution)/shard_map/ppermute | solution.py:128
  18.9 10.6 %collective-permute-done = f32[2,48,2304]{2,1,0:T(8,128)S(1)} collective-permute-done((f32[2,48,2304]{2,1,0:T(8,128)S(1)}, f32[2,48,2304]{2,1,0:T(8,128)S(1)}, u32[]{:S(2)}, u32[]{:S(2)}) %collective-permute-start) | collective-permute-done | bytes 884768 | tf_op jit(solution)/shard_map/ppermute | solution.py:128
  29.5 4.6 %collective-permute-start.1 = (f32[2,48,2304]{2,1,0:T(8,128)S(1)}, f32[2,48,2304]{2,1,0:T(8,128)S(1)}, u32[]{:S(2)}, u32[]{:S(2)}) collective-permute-start(f32[2,48,2304]{2,1,0:T(8,128)S(1)} %collective-permute-done), channel_id=1, source_target_pairs={{2,0},{4,2},{6,4},{8,6},{10,8},{12,10},{14,12},{16,14},{18,16},{20... | collective-permute-start | bytes 2654216 | tf_op jit(solution)/shard_map/ppermute | solution.py:128
  34.1 0.6 dynamic_slice.9
  35.4 0.0 copy-start
  35.4 0.0 copy-start.1
  35.4 0.0 copy-start.2
  35.5 0.0 copy-start.3
  35.5 9.2 %collective-permute-done.1 = f32[2,48,2304]{2,1,0:T(8,128)S(1)} collective-permute-done((f32[2,48,2304]{2,1,0:T(8,128)S(1)}, f32[2,48,2304]{2,1,0:T(8,128)S(1)}, u32[]{:S(2)}, u32[]{:S(2)}) %collective-permute-start.1) | collective-permute-done | bytes 884768 | tf_op jit(solution)/shard_map/ppermute | solution.py:128
  44.7 1.7 %pad_maximum_fusion.visit_ref = f32[6,48,2304]{2,1,0:T(8,128)} fusion(f32[2,48,2304]{2,1,0:T(8,128)S(1)} %collective-permute-done.1, f32[2,48,2304]{2,1,0:T(8,128)S(1)} %collective-permute-done, f32[2,48,2304]{2,1,0:T(8,128)S(1)} %all_gather.3), kind=kLoop, calls=%fused_computation | loop fusion | flops 1327104 | bytes 5308416 | tf_op jit(solution)/shard_map/concatenate | solution.py:144
  46.4 0.0 copy-done
  46.4 0.0 copy-done.1
  46.4 0.0 copy-done.2
  46.4 0.0 copy-done.3
  46.4 19.5 %shard_map.64 = f32[48,2304]{1,0:T(8,128)S(1)} custom-call(f32[48,2304]{1,0:T(8,128)S(1)} %dynamic-slice_bitcast_fusion.mine_ref, f32[6,48,2304]{2,1,0:T(8,128)} %pad_maximum_fusion.visit_ref, f32[48,1152]{1,0:T(8,128)S(1)} %copy-done.2, f32[3,24,1152]{2,1,0:T(8,128)S(1)} %copy-done.1, bf16[48,144]{1,0:T(8,128)(2,1)S(1)} %copy-done.3, f32[48,2304]{1,0:T(8,128)S(1)} %copy-done), custom_call_target="tpu_custom_call" | custom-call | tf_op jit(solution)/shard_map/pallas_call | solution.py:132
  65.9 8.7 %all_to_all.4 = f32[2,1,1,24,2304]{4,3,2,1,0:T(8,128)S(1)} all-to-all(f32[2,1,1,24,2304]{4,3,2,1,0:T(8,128)S(1)} %bitcast.7), channel_id=1, replica_groups=mesh['band'=16,'grid'=2] {'grid'}, dimensions={0} | all-to-all | bytes 884736 | tf_op jit(solution)/shard_map/all_to_all | solution.py:146
  74.6 0.8 %copy.9 = f32[2,24,2304]{2,1,0:T(8,128)} copy(f32[2,24,2304]{2,1,0:T(8,128)S(1)} %bitcast.8) | data formatting | bytes 884736
  (2 shorter events, 0.1 us)
Async XLA Ops:
  15.6 13.9 %collective-permute-start = (f32[2,48,2304]{2,1,0:T(8,128)S(1)}, f32[2,48,2304]{2,1,0:T(8,128)S(1)}, u32[]{:S(2)}, u32[]{:S(2)}) collective-permute-start(f32[2,48,2304]{2,1,0:T(8,128)S(1)} %all_gather.3), channel_id=1, source_target_pairs={{2,0},{4,2},{6,4},{8,6},{10,8},{12,10},{14,12},{16,14},{18,16},{20... | collective-permute-start | bytes 2654216 | tf_op jit(solution)/shard_map/ppermute | solution.py:128
  29.5 15.2 %collective-permute-start.1 = (f32[2,48,2304]{2,1,0:T(8,128)S(1)}, f32[2,48,2304]{2,1,0:T(8,128)S(1)}, u32[]{:S(2)}, u32[]{:S(2)}) collective-permute-start(f32[2,48,2304]{2,1,0:T(8,128)S(1)} %collective-permute-done), channel_id=1, source_target_pairs={{2,0},{4,2},{6,4},{8,6},{10,8},{12,10},{14,12},{16,14},{18,16},{20... | collective-permute-start | bytes 2654216 | tf_op jit(solution)/shard_map/ppermute | solution.py:128
  35.4 11.0 %copy-start = (f32[48,2304]{1,0:T(8,128)S(1)}, f32[48,2304]{1,0:T(8,128)}, u32[]{:S(2)}) copy-start(f32[48,2304]{1,0:T(8,128)} %constant.28.clone.coulomb) | copy-start | bytes 1327108
  35.4 11.0 %copy-start.1 = (f32[3,24,1152]{2,1,0:T(8,128)S(1)}, f32[3,24,1152]{2,1,0:T(8,128)}, u32[]{:S(2)}) copy-start(f32[3,24,1152]{2,1,0:T(8,128)} %constant.26.clone.along_y) | copy-start | bytes 995332
  35.4 11.0 %copy-start.2 = (f32[48,1152]{1,0:T(8,128)S(1)}, f32[48,1152]{1,0:T(8,128)}, u32[]{:S(2)}) copy-start(f32[48,1152]{1,0:T(8,128)} %constant.25.clone.along_z) | copy-start | bytes 663556
  35.5 10.9 %copy-start.3 = (bf16[48,144]{1,0:T(8,128)(2,1)S(1)}, bf16[48,144]{1,0:T(8,128)(2,1)}, u32[]{:S(2)}) copy-start(bf16[48,144]{1,0:T(8,128)(2,1)} %constant.27.clone.along_x) | copy-start | bytes 41476
where the time goes:
time: 75.6 us; the launch traced here: 75.4 us
  blocking collectives  22.5 us (30%)
  waiting for transfers between devices  19.8 us (26%)
  Pallas kernels  19.5 us (26%)
  starting transfers between devices  7.98 us (11%)
  other arithmetic  2.87 us (4%)
  local copies, waits for them, and re-layouts  2.07 us (3%)
  between operations  0.76 us (1%)
    ppermute x2, waiting for transfers between devices, per_device(): blocks.append(lax.ppermute(blocks[-1], 'band', route))  19.8 us
    pallas_call x1, Pallas kernels, per_device(): pl.pallas_call(kernel, out_shape=jax.ShapeDtypeStruct((N, plane), jnp.flo...  19.5 us
    all_gather x1, blocking collectives, per_device(): lax.all_gather(orbitals * root[:, None, None], 'grid', axis=1, tiled=True)  13.8 us
    all_to_all x1, blocking collectives, per_device(): result = lax.all_to_all(result, 'grid', 0, 1)  8.7 us
    ppermute x2, starting transfers between devices, per_device(): blocks.append(lax.ppermute(blocks[-1], 'band', route))  7.98 us
    concatenate x1, other arithmetic, per_device(): jnp.concatenate(blocks)  1.73 us
  transfers between devices with their start and end apart: 2, of which 2 were waited for; matrix products, arithmetic and copies ran while one was open for 1% of the time, Pallas kernels for 0%

commit v1 on v0

v1 whole, which is shorter than its diff:
```python
import jax
import jax.numpy as jnp
import numpy as np
from jax import lax
from jax.experimental import pallas as pl
from jax.experimental.pallas import tpu as pltpu
from jax.sharding import PartitionSpec as P

N = 48
HALF = N // 2
PLANE = N * N
COLS = PLANE // 2
STOPS = 3
PAD = 8
SIDE = 3 * HALF + PAD
MESH = pl.DeviceIdType.MESH
CUTS = [(0, 256), (256, 256), (512, 256), (768, 256), (1024, 128)]


def cas(product, length):
    angle = (product % length) * (2.0 * np.pi / length)
    return np.cos(angle) + np.sin(angle)


def tables():
    i, h = np.arange(N), np.arange(HALF)
    along_z = np.tile(cas(i[:, None] * i[None, :], N), (1, HALF))
    even = cas(2 * h[:, None] * h[None, :], N)
    odd = cas(h[:, None] * (2 * h[None, :] + 1), N)
    along_y = np.stack([np.repeat(m, N, axis=1) for m in (even, odd, odd.T)])
    square = np.where(i <= HALF, i, i - N).astype(np.float64) ** 2
    order = np.concatenate([i[0::2], i[1::2]])
    total = square[:, None, None] + square[order][None, :, None] + square[None, None, :]
    coulomb = np.where(total > 0, 24.0 * 24.0 / np.pi / np.where(total > 0, total, 1.0), 0.0)
    coulomb = coulomb.reshape(N, PLANE) * (-0.25 / N**3)
    along_x = cas(i[:, None] * i[None, :], N)
    x_high = along_x.astype(np.float32).astype(jnp.bfloat16)
    x_low = (along_x - x_high.astype(np.float64)).astype(np.float32).astype(jnp.bfloat16)
    there, back = [], []
    for place in range(2):
        halves = [slice(s * HALF, (s + 1) * HALF) for s in (place, 1 - place)]
        pad = np.zeros((N, PAD), x_high.dtype)
        there.append(
            np.concatenate(
                [b for s in halves for b in (x_high[:, s], x_high[:, s], x_low[:, s], pad)], axis=1
            )
        )
        high, low = (np.concatenate([m[s] for s in halves]) for m in (x_high, x_low))
        back.append(np.concatenate([high, high, low], axis=1))
    return (
        along_z.astype(np.float32),
        along_y.astype(np.float32),
        np.stack(there),
        np.stack(back),
        coulomb.astype(np.float32),
    )


def split(value):
    high = value.astype(jnp.bfloat16)
    return high, (value - high.astype(jnp.float32)).astype(jnp.bfloat16)


def split32(value):
    high = value.astype(jnp.bfloat16).astype(jnp.float32)
    return high, value - high


def dot(a, b):
    return jnp.dot(a, b, preferred_element_type=jnp.float32)


def kernel(
    psi, occ, along_z, along_y, there, back, coulomb,
    out, buf, w_high, w_low, slabs, lhs, xrhs, acc, send, recv, out_send, out_recv,
):
    band, grid = lax.axis_index("band"), lax.axis_index("grid")
    devices = lax.axis_size("band")
    left = {"band": lax.rem(band + devices - 1, devices), "grid": grid}
    right = {"band": lax.rem(band + 1, devices), "grid": grid}
    across = {"band": band, "grid": 1 - grid}
    odd = lax.rem(band, 2) == 1

    barrier = pltpu.get_barrier_semaphore()
    for device in (across, right):
        pl.semaphore_signal(barrier, inc=1, device_id=device, device_id_type=MESH)

    def root(k):
        return jnp.sqrt(jnp.full((1, 128), occ[k], jnp.float32))

    for k in range(2):
        factor = root(k)
        for start in range(0, PLANE, 128):
            at = slice(start, start + 128)
            buf[0, k, 0, :, at] = psi[k, :, at] * factor

    def copy(number, k, source, target, device):
        return pltpu.make_async_remote_copy(
            src_ref=buf.at[source[0], k, source[1]],
            dst_ref=buf.at[target[0], k, target[1]],
            send_sem=send.at[number, k],
            recv_sem=recv.at[target[0], target[1], k],
            device_id=device,
            device_id_type=MESH,
        )

    swap = [copy(0, k, (0, 0), (0, 1), across) for k in (1 - grid, grid)]
    own = [copy(1, k, (0, 0), (1, 0), left) for k in range(2)]
    own_on = [copy(2, k, (1, 0), (2, 0), left) for k in range(2)]
    other = [copy(3, k, (0, 1), (1, 1), left) for k in range(2)]
    other_on = [copy(4, k, (1, 1), (2, 1), left) for k in range(2)]
    other_swap = [copy(5, k, (2, 0), (2, 1), across) for k in range(2)]

    def start(copies):
        for c in copies:
            c.start()

    def arrived(copies):
        for c in copies:
            c.wait_recv()

    def build(m):
        @pl.loop(0, HALF)
        def _(y):
            rows = pl.ds(pl.multiple_of(y * N, 16), N)
            high, low = split(along_z[...] * along_y[m, pl.ds(y, 1), :])
            w_high[m, rows, :] = high
            w_low[m, rows, :] = low

    def forward(stop, side):
        for first in range(0, COLS, 128):
            cols = [slice(s, s + 128) for s in (first, COLS + first)]
            low_y, high_y = (
                jnp.concatenate([buf[0, grid, side, :, c] * buf[stop, k, side, :, c] for k in range(2)])
                for c in cols
            )
            for parity, value in enumerate((low_y + high_y, low_y - high_y)):
                slabs[parity, :N, cols[0]], slabs[parity, N:, cols[0]] = split(value)
        for parity in range(2):
            for first, size in CUTS:
                cut = slice(first, first + size)
                both = dot(slabs[parity], w_high[parity, :, cut])
                value = both[:N] + both[N:] + dot(slabs[parity, :N, :], w_low[parity, :, cut])
                high, low = split32(value)
                to = slice(parity * COLS + first, parity * COLS + first + size)
                for k in range(2):
                    rows = slice(k * HALF, (k + 1) * HALF)
                    pad = jnp.zeros((PAD, size), jnp.float32)
                    block = jnp.concatenate([high[rows], low[rows], high[rows], pad])
                    xrhs[stop, k, side * SIDE : (side + 1) * SIDE, to] = block.astype(jnp.bfloat16)

    def finish(stop):
        for parity in range(2):
            for first, size in CUTS:
                at = slice(parity * COLS + first, parity * COLS + first + size)
                for k in range(2):
                    work = dot(there[grid], xrhs[stop, k, :, at]) * coulomb[:, at]
                    high, low = split(work)
                    work = dot(back[grid], jnp.concatenate([high, low, high]))
                    high, low = split(work)
                    lhs[parity, k * N : (k + 1) * N, first : first + size] = high
                    lhs[parity, (k + 2) * N : (k + 3) * N, first : first + size] = low

        def yz(which, parity, cut):
            both = dot(lhs[parity], w_high[which, :, cut])
            return both[: 2 * N] + both[2 * N :] + dot(lhs[parity, : 2 * N, :], w_low[which, :, cut])

        sent = []
        scale = 1.0 / root(grid)[:, :1] if stop == STOPS - 1 else None
        for first, size in CUTS:
            cols = [slice(s, s + size) for s in (first, COLS + first)]
            even, odd_y = yz(0, 0, cols[0]), yz(2, 1, cols[0])
            for at, value in zip(cols, (even + odd_y, even - odd_y)):
                for side in range(2):
                    rows = slice(side * HALF, (side + 1) * HALF)
                    term = sum(
                        value[k * N + side * HALF : k * N + (side + 1) * HALF] * buf[stop, k, side, :, at]
                        for k in range(2)
                    )
                    if stop > 0:
                        term = term + acc[rows, at]
                    if scale is None:
                        acc[rows, at] = term
                    elif side == 0:
                        out[grid, :, at] = term * scale
                    else:
                        acc[rows, at] = term * scale
                if scale is not None:
                    sent.append(
                        pltpu.make_async_remote_copy(
                            src_ref=acc.at[pl.ds(HALF, HALF), pl.ds(at.start, size)],
                            dst_ref=out.at[grid, :, pl.ds(at.start, size)],
                            send_sem=out_send.at[len(sent)],
                            recv_sem=out_recv.at[len(sent)],
                            device_id=across,
                            device_id_type=MESH,
                        )
                    )
                    sent[-1].start()
        return sent

    pl.semaphore_wait(barrier, 2)
    start(swap)
    start(own)
    build(0)
    build(1)
    forward(0, 0)
    arrived(own)
    start(own_on)
    forward(1, 0)
    build(2)
    arrived(swap)
    start(other)
    arrived(own_on)

    @pl.when(odd)
    def _():
        start(other_swap)

    forward(0, 1)
    finish(0)
    forward(2, 0)
    arrived(other)

    @pl.when(odd)
    def _():
        start(other_on)

    forward(1, 1)
    finish(1)
    arrived(other_on)
    forward(2, 1)
    sent = finish(2)
    for c in swap + own + own_on + other:
        c.wait_send()

    @pl.when(odd)
    def _():
        for c in other_on + other_swap:
            c.wait_send()

    for c in sent:
        c.wait()


def per_device(orbitals, occupation):
    count, slab, plane = orbitals.shape
    vmem = pl.BlockSpec(memory_space=pltpu.VMEM)
    return pl.pallas_call(
        kernel,
        out_shape=jax.ShapeDtypeStruct((count, slab, plane), jnp.float32),
        in_specs=[vmem, pl.BlockSpec(memory_space=pltpu.SMEM)] + [vmem] * 5,
        out_specs=vmem,
        scratch_shapes=[
            pltpu.VMEM((STOPS, count, 2, slab, plane), jnp.float32),
            pltpu.VMEM((3, COLS, COLS), jnp.bfloat16),
            pltpu.VMEM((3, COLS, COLS), jnp.bfloat16),
            pltpu.VMEM((2, 2 * N, COLS), jnp.bfloat16),
            pltpu.VMEM((2, 4 * N, COLS), jnp.bfloat16),
            pltpu.VMEM((STOPS, count, 2 * SIDE, plane), jnp.bfloat16),
            pltpu.VMEM((N, plane), jnp.float32),
            pltpu.SemaphoreType.DMA((6, count)),
            pltpu.SemaphoreType.DMA((STOPS, 2, count)),
            pltpu.SemaphoreType.DMA((2 * len(CUTS),)),
            pltpu.SemaphoreType.DMA((2 * len(CUTS),)),
        ],
        compiler_params=pltpu.CompilerParams(
            vmem_limit_bytes=50 << 20, collective_id=0, has_side_effects=True
        ),
    )(orbitals, occupation, *[jnp.asarray(t) for t in tables()])


def solution(mesh):
    placed = (P("band", "grid", None), P("band"))
    return jax.shard_map(
        per_device, mesh=mesh, in_specs=placed, out_specs=P("band", "grid", None), check_vma=False
    )
```

time: 75.6 us -> 50 us (0.66)
  Pallas kernels: 19.5 us -> 42.7 us
  blocking collectives: 22.5 us -> 0 us
  waiting for transfers between devices: 19.8 us -> 0 us
  starting transfers between devices: 7.98 us -> 0 us
  local copies, waits for them, and re-layouts: 2.07 us -> 6.95 us
  other arithmetic: 2.87 us -> 0 us
    pallas_call x1, Pallas kernels: 19.5 us -> 42.7 us  [per_device(): pl.pallas_call(kernel, out_shape=jax.ShapeDtypeStruct((count, slab, plane...]
    ppermute x2 -> x0, waiting for transfers between devices: 19.8 us -> none  [per_device(): blocks.append(lax.ppermute(blocks[-1], 'band', route))]
    all_gather x1 -> x0, blocking collectives: 13.8 us -> none  [per_device(): lax.all_gather(orbitals * root[:, None, None], 'grid', axis=1, tiled=True)]
    all_to_all x1 -> x0, blocking collectives: 8.7 us -> none  [per_device(): result = lax.all_to_all(result, 'grid', 0, 1)]
    ppermute x2 -> x0, starting transfers between devices: 7.98 us -> none  [per_device(): blocks.append(lax.ppermute(blocks[-1], 'band', route))]
    unnamed x9 -> x15, local copies, waits for them, and re-layouts: 0.79 us -> 6.95 us
    concatenate x1 -> x0, other arithmetic: 1.73 us -> none  [per_device(): jnp.concatenate(blocks)]
    mul x2 -> x0, other arithmetic: 1.15 us -> none  [the longest x1 1.11 us: per_device(): orbitals * root[:, None, None]]
  transfers between devices with their start and end apart: 2 -> 0, of which waited for: 2 -> 0; matrix products, arithmetic and copies ran while one was open for 1% -> 0% of each run, Pallas kernels for 0% -> 0%
where the time goes in v1:
time: 50 us; the launch traced here: 49.6 us
  Pallas kernels  42.7 us (85%)
  local copies, waits for them, and re-layouts  6.95 us (14%)
    pallas_call x1, Pallas kernels, per_device(): pl.pallas_call(kernel, out_shape=jax.ShapeDtypeStruct((count, slab, plane...  42.7 us
    unnamed x15, local copies, waits for them, and re-layouts  6.95 us

profile of v1, /device:TPU:0, one launch (start us, length us, event | category | flops | bytes accessed | tf_op | source)
XLA Modules:
  0.0 49.6 jit_solution(11587786167339725628)
XLA Ops:
  0.0 0.0 copy-start
  0.0 1.0 %copy-done = f32[2,24,2304]{2,1,0:T(8,128)S(1)} copy-done((f32[2,24,2304]{2,1,0:T(8,128)S(1)}, f32[2,24,2304]{2,1,0:T(8,128)}, u32[]{:S(2)}) %copy-start) | copy-done | bytes 442392
  1.0 0.0 copy-start.1
  1.0 1.0 %copy-done.1 = f32[48,2304]{1,0:T(8,128)S(1)} copy-done((f32[48,2304]{1,0:T(8,128)S(1)}, f32[48,2304]{1,0:T(8,128)}, u32[]{:S(2)}) %copy-start.1) | copy-done | bytes 442392
  2.0 0.0 copy-start.2
  2.0 1.0 %copy-done.2 = f32[3,24,1152]{2,1,0:T(8,128)S(1)} copy-done((f32[3,24,1152]{2,1,0:T(8,128)S(1)}, f32[3,24,1152]{2,1,0:T(8,128)}, u32[]{:S(2)}) %copy-start.2) | copy-done | bytes 331800
  3.0 0.0 copy-start.3
  3.0 0.9 %copy-done.3 = f32[48,1152]{1,0:T(8,128)S(1)} copy-done((f32[48,1152]{1,0:T(8,128)S(1)}, f32[48,1152]{1,0:T(8,128)}, u32[]{:S(2)}) %copy-start.3) | copy-done | bytes 221208
  3.9 0.0 copy-start.4
  3.9 0.8 %copy-done.4 = bf16[2,48,144]{2,1,0:T(8,128)(2,1)S(1)} copy-done((bf16[2,48,144]{2,1,0:T(8,128)(2,1)S(1)}, bf16[2,48,144]{2,1,0:T(8,128)(2,1)}, u32[]{:S(2)}) %copy-start.4) | copy-done | bytes 27672
  4.7 0.0 copy-start.5
  4.7 0.8 %copy-done.5 = bf16[2,48,160]{2,1,0:T(8,128)(2,1)S(1)} copy-done((bf16[2,48,160]{2,1,0:T(8,128)(2,1)S(1)}, bf16[2,48,160]{2,1,0:T(8,128)(2,1)}, u32[]{:S(2)}) %copy-start.5) | copy-done | bytes 30744
  5.5 0.0 copy-start.6
  5.5 0.7 %copy-done.6 = f32[2]{0:T(128)S(1)} copy-done((f32[2]{0:T(128)S(1)}, f32[2]{0:T(128)}, u32[]{:S(2)}) %copy-start.6) | copy-done | bytes 32
  6.2 42.7 %shard_map.73 = f32[2,24,2304]{2,1,0:T(8,128)S(1)} custom-call(f32[2,24,2304]{2,1,0:T(8,128)S(1)} %copy-done, f32[2]{0:T(128)S(1)} %copy-done.6, f32[48,1152]{1,0:T(8,128)S(1)} %copy-done.3, f32[3,24,1152]{2,1,0:T(8,128)S(1)} %copy-done.2, bf16[2,48,160]{2,1,0:T(8,128)(2,1)S(1)} %copy-done.5, bf16[2,48,144]{2,1,0:T(8,128)(2,1)S(1)} %copy-done.4, ...), custom_call_target="tpu_custom_call" | custom-call | tf_op jit(solution)/shard_map/pallas_call | solution.py:249
  48.9 0.8 %copy.9 = f32[2,24,2304]{2,1,0:T(8,128)} copy(f32[2,24,2304]{2,1,0:T(8,128)S(1)} %shard_map.73) | data formatting | bytes 884736
Async XLA Ops:
  0.0 1.0 %copy-start = (f32[2,24,2304]{2,1,0:T(8,128)S(1)}, f32[2,24,2304]{2,1,0:T(8,128)}, u32[]{:S(2)}) copy-start(f32[2,24,2304]{2,1,0:T(8,128)} %psi.1) | copy-start | bytes 1327108
  1.0 1.0 %copy-start.1 = (f32[48,2304]{1,0:T(8,128)S(1)}, f32[48,2304]{1,0:T(8,128)}, u32[]{:S(2)}) copy-start(f32[48,2304]{1,0:T(8,128)} %constant.14.clone.coulomb) | copy-start | bytes 1327108
  2.0 1.0 %copy-start.2 = (f32[3,24,1152]{2,1,0:T(8,128)S(1)}, f32[3,24,1152]{2,1,0:T(8,128)}, u32[]{:S(2)}) copy-start(f32[3,24,1152]{2,1,0:T(8,128)} %constant.11.clone.along_y) | copy-start | bytes 995332
  3.0 0.9 %copy-start.3 = (f32[48,1152]{1,0:T(8,128)S(1)}, f32[48,1152]{1,0:T(8,128)}, u32[]{:S(2)}) copy-start(f32[48,1152]{1,0:T(8,128)} %constant.10.clone.along_z) | copy-start | bytes 663556
  3.9 0.8 %copy-start.4 = (bf16[2,48,144]{2,1,0:T(8,128)(2,1)S(1)}, bf16[2,48,144]{2,1,0:T(8,128)(2,1)}, u32[]{:S(2)}) copy-start(bf16[2,48,144]{2,1,0:T(8,128)(2,1)} %constant.13.clone.back) | copy-start | bytes 82948
  4.7 0.8 %copy-start.5 = (bf16[2,48,160]{2,1,0:T(8,128)(2,1)S(1)}, bf16[2,48,160]{2,1,0:T(8,128)(2,1)}, u32[]{:S(2)}) copy-start(bf16[2,48,160]{2,1,0:T(8,128)(2,1)} %constant.12.clone.there) | copy-start | bytes 92164
  5.5 0.7 %copy-start.6 = (f32[2]{0:T(128)S(1)}, f32[2]{0:T(128)}, u32[]{:S(2)}) copy-start(f32[2]{0:T(128)} %occ.1) | copy-start | bytes 28

commit v2 on v1

--- a/solution.py
+++ b/solution.py
@@ -71,9 +71,15 @@
 
 
 def kernel(
-    psi, occ, along_z, along_y, there, back, coulomb,
-    out, buf, w_high, w_low, slabs, lhs, xrhs, acc, send, recv, out_send, out_recv,
+    occ, psi_in, z_in, y_in, there_in, back_in, coulomb_in,
+    out, psi, along_z, along_y, there, back, coulomb,
+    buf, w_high, w_low, slabs, lhs, xrhs, acc, load, send, recv, out_send, out_recv,
 ):
+    sources = (psi_in, z_in, y_in, there_in, back_in, coulomb_in)
+    targets = (psi, along_z, along_y, there, back, coulomb)
+    loads = [pltpu.make_async_copy(a, b, load.at[i]) for i, (a, b) in enumerate(zip(sources, targets))]
+    for c in loads:
+        c.start()
     band, grid = lax.axis_index("band"), lax.axis_index("grid")
     devices = lax.axis_size("band")
     left = {"band": lax.rem(band + devices - 1, devices), "grid": grid}
@@ -88,6 +94,7 @@
     def root(k):
         return jnp.sqrt(jnp.full((1, 128), occ[k], jnp.float32))
 
+    loads[0].wait()
     for k in range(2):
         factor = root(k)
         for start in range(0, PLANE, 128):
@@ -127,65 +134,76 @@
             w_high[m, rows, :] = high
             w_low[m, rows, :] = low
 
-    def forward(stop, side):
+    def forward(*parts):
+        rows = N * len(parts)
         for first in range(0, COLS, 128):
             cols = [slice(s, s + 128) for s in (first, COLS + first)]
             low_y, high_y = (
-                jnp.concatenate([buf[0, grid, side, :, c] * buf[stop, k, side, :, c] for k in range(2)])
+                jnp.concatenate(
+                    [
+                        buf[0, grid, side, :, c] * buf[stop, k, side, :, c]
+                        for stop, side in parts
+                        for k in range(2)
+                    ]
+                )
                 for c in cols
             )
             for parity, value in enumerate((low_y + high_y, low_y - high_y)):
-                slabs[parity, :N, cols[0]], slabs[parity, N:, cols[0]] = split(value)
+                slabs[parity, :rows, cols[0]], slabs[parity, rows:, cols[0]] = split(value)
         for parity in range(2):
             for first, size in CUTS:
                 cut = slice(first, first + size)
                 both = dot(slabs[parity], w_high[parity, :, cut])
-                value = both[:N] + both[N:] + dot(slabs[parity, :N, :], w_low[parity, :, cut])
+                value = both[:rows] + both[rows:] + dot(slabs[parity, :rows, :], w_low[parity, :, cut])
                 high, low = split32(value)
                 to = slice(parity * COLS + first, parity * COLS + first + size)
-                for k in range(2):
-                    rows = slice(k * HALF, (k + 1) * HALF)
-                    pad = jnp.zeros((PAD, size), jnp.float32)
-                    block = jnp.concatenate([high[rows], low[rows], high[rows], pad])
-                    xrhs[stop, k, side * SIDE : (side + 1) * SIDE, to] = block.astype(jnp.bfloat16)
-
-    def finish(stop):
-        for parity in range(2):
-            for first, size in CUTS:
-                at = slice(parity * COLS + first, parity * COLS + first + size)
-                for k in range(2):
-                    work = dot(there[grid], xrhs[stop, k, :, at]) * coulomb[:, at]
-                    high, low = split(work)
-                    work = dot(back[grid], jnp.concatenate([high, low, high]))
-                    high, low = split(work)
-                    lhs[parity, k * N : (k + 1) * N, first : first + size] = high
-                    lhs[parity, (k + 2) * N : (k + 3) * N, first : first + size] = low
+                pad = jnp.zeros((PAD, size), jnp.float32)
+                for n, (stop, side) in enumerate(parts):
+                    for k in range(2):
+                        at = slice((2 * n + k) * HALF, (2 * n + k + 1) * HALF)
+                        block = jnp.concatenate([high[at], low[at], high[at], pad])
+                        xrhs[stop, k, side * SIDE : (side + 1) * SIDE, to] = block.astype(jnp.bfloat16)
+
+    def finish(stops, hook=None):
+        pairs = [(stop, k) for stop in stops for k in range(2)]
+        rows = N * len(pairs)
+        for first in range(0, PLANE, 256):
+            at = slice(first, first + 256)
+            for n, (stop, k) in enumerate(pairs):
+                work = dot(there[grid], xrhs[stop, k, :, at]) * coulomb[:, at]
+                high, low = split(work)
+                work = dot(back[grid], jnp.concatenate([high, low, high]))
+                high, low = split(work)
+                lhs[n * N : (n + 1) * N, at] = high
+                lhs[rows + n * N : rows + (n + 1) * N, at] = low
 
         def yz(which, parity, cut):
-            both = dot(lhs[parity], w_high[which, :, cut])
-            return both[: 2 * N] + both[2 * N :] + dot(lhs[parity, : 2 * N, :], w_low[which, :, cut])
-
+            half = slice(parity * COLS, (parity + 1) * COLS)
+            both = dot(lhs[: 2 * rows, half], w_high[which, :, cut])
+            return both[:rows] + both[rows:] + dot(lhs[:rows, half], w_low[which, :, cut])
+
+        last = STOPS - 1 in stops
+        scale = 1.0 / root(grid)[:, :1] if last else None
         sent = []
-        scale = 1.0 / root(grid)[:, :1] if stop == STOPS - 1 else None
-        for first, size in CUTS:
+        for number, (first, size) in enumerate(CUTS):
             cols = [slice(s, s + size) for s in (first, COLS + first)]
             even, odd_y = yz(0, 0, cols[0]), yz(2, 1, cols[0])
             for at, value in zip(cols, (even + odd_y, even - odd_y)):
                 for side in range(2):
-                    rows = slice(side * HALF, (side + 1) * HALF)
+                    part = slice(side * HALF, (side + 1) * HALF)
                     term = sum(
-                        value[k * N + side * HALF : k * N + (side + 1) * HALF] * buf[stop, k, side, :, at]
-                        for k in range(2)
+                        value[n * N + side * HALF : n * N + (side + 1) * HALF] * buf[stop, k, side, :, at]
+                        for n, (stop, k) in enumerate(pairs)
                     )
-                    if stop > 0:
-                        term = term + acc[rows, at]
-                    if scale is None:
-                        acc[rows, at] = term
+                    if 0 not in stops:
+                        term = term + acc[part, at]
+                    if not last:
+                        acc[part, at] = term
                     elif side == 0:
                         out[grid, :, at] = term * scale
                     else:
-                        acc[rows, at] = term * scale
-                if scale is not None:
+                        acc[part, at] = term * scale
+                if last:
                     sent.append(
                         pltpu.make_async_remote_copy(
                             src_ref=acc.at[pl.ds(HALF, HALF), pl.ds(at.start, size)],
@@ -197,18 +215,30 @@
                         )
                     )
                     sent[-1].start()
+            if hook is not None and number == 2:
+                hook()
         return sent
+
+    def pass_other():
+        arrived(other)
+
+        @pl.when(odd)
+        def _():
+            start(other_on)
 
     pl.semaphore_wait(barrier, 2)
     start(swap)
     start(own)
+    loads[1].wait()
+    loads[2].wait()
     build(0)
     build(1)
-    forward(0, 0)
+    build(2)
+    for c in loads[3:]:
+        c.wait()
     arrived(own)
     start(own_on)
-    forward(1, 0)
-    build(2)
+    forward((0, 0), (1, 0))
     arrived(swap)
     start(other)
     arrived(own_on)
@@ -217,20 +247,11 @@
     def _():
         start(other_swap)
 
-    forward(0, 1)
-    finish(0)
-    forward(2, 0)
-    arrived(other)
-
-    @pl.when(odd)
-    def _():
-        start(other_on)
-
-    forward(1, 1)
-    finish(1)
+    forward((0, 1), (2, 0))
+    finish([0], pass_other)
     arrived(other_on)
-    forward(2, 1)
-    sent = finish(2)
+    forward((1, 1), (2, 1))
+    sent = finish([1, 2])
     for c in swap + own + own_on + other:
         c.wait_send()
 
@@ -246,19 +267,22 @@
 def per_device(orbitals, occupation):
     count, slab, plane = orbitals.shape
     vmem = pl.BlockSpec(memory_space=pltpu.VMEM)
+    operands = [orbitals] + [jnp.asarray(t) for t in tables()]
     return pl.pallas_call(
         kernel,
         out_shape=jax.ShapeDtypeStruct((count, slab, plane), jnp.float32),
-        in_specs=[vmem, pl.BlockSpec(memory_space=pltpu.SMEM)] + [vmem] * 5,
+        in_specs=[pl.BlockSpec(memory_space=pltpu.SMEM)] + [pl.BlockSpec(memory_space=pltpu.HBM)] * 6,
         out_specs=vmem,
-        scratch_shapes=[
+        scratch_shapes=[pltpu.VMEM(t.shape, t.dtype) for t in operands]
+        + [
             pltpu.VMEM((STOPS, count, 2, slab, plane), jnp.float32),
             pltpu.VMEM((3, COLS, COLS), jnp.bfloat16),
             pltpu.VMEM((3, COLS, COLS), jnp.bfloat16),
-            pltpu.VMEM((2, 2 * N, COLS), jnp.bfloat16),
             pltpu.VMEM((2, 4 * N, COLS), jnp.bfloat16),
+            pltpu.VMEM((8 * N, PLANE), jnp.bfloat16),
             pltpu.VMEM((STOPS, count, 2 * SIDE, plane), jnp.bfloat16),
             pltpu.VMEM((N, plane), jnp.float32),
+            pltpu.SemaphoreType.DMA((6,)),
             pltpu.SemaphoreType.DMA((6, count)),
             pltpu.SemaphoreType.DMA((STOPS, 2, count)),
             pltpu.SemaphoreType.DMA((2 * len(CUTS),)),
@@ -267,7 +291,7 @@
         compiler_params=pltpu.CompilerParams(
             vmem_limit_bytes=50 << 20, collective_id=0, has_side_effects=True
         ),
-    )(orbitals, occupation, *[jnp.asarray(t) for t in tables()])
+    )(occupation, *operands)
 
 
 def solution(mesh):

time: 50 us -> 47.6 us (0.952)
  Pallas kernels: 42.7 us -> 40 us
    pallas_call x1, Pallas kernels: 42.7 us -> 40 us  [per_device(): pl.pallas_call(kernel, out_shape=jax.ShapeDtypeStruct((count, slab, plane...]
where the time goes in v2:
time: 47.6 us; the launch traced here: 47 us
  Pallas kernels  40 us (84%)
  local copies, waits for them, and re-layouts  6.95 us (15%)
    pallas_call x1, Pallas kernels, per_device(): pl.pallas_call(kernel, out_shape=jax.ShapeDtypeStruct((count, slab, plane...  40 us
    unnamed x15, local copies, waits for them, and re-layouts  6.95 us

profile of v2, /device:TPU:0, one launch (start us, length us, event | category | flops | bytes accessed | tf_op | source)
XLA Modules:
  0.0 47.0 jit_solution(3996980978739100046)
XLA Ops:
  0.0 0.0 copy-start
  0.0 1.0 %copy-done = f32[2,24,2304]{2,1,0:T(8,128)S(1)} copy-done((f32[2,24,2304]{2,1,0:T(8,128)S(1)}, f32[2,24,2304]{2,1,0:T(8,128)}, u32[]{:S(2)}) %copy-start) | copy-done | bytes 442392
  1.0 0.0 copy-start.1
  1.0 1.0 %copy-done.1 = f32[48,2304]{1,0:T(8,128)S(1)} copy-done((f32[48,2304]{1,0:T(8,128)S(1)}, f32[48,2304]{1,0:T(8,128)}, u32[]{:S(2)}) %copy-start.1) | copy-done | bytes 442392
  2.0 0.0 copy-start.2
  2.0 1.0 %copy-done.2 = f32[3,24,1152]{2,1,0:T(8,128)S(1)} copy-done((f32[3,24,1152]{2,1,0:T(8,128)S(1)}, f32[3,24,1152]{2,1,0:T(8,128)}, u32[]{:S(2)}) %copy-start.2) | copy-done | bytes 331800
  3.0 0.0 copy-start.3
  3.0 0.9 %copy-done.3 = f32[48,1152]{1,0:T(8,128)S(1)} copy-done((f32[48,1152]{1,0:T(8,128)S(1)}, f32[48,1152]{1,0:T(8,128)}, u32[]{:S(2)}) %copy-start.3) | copy-done | bytes 221208
  3.9 0.0 copy-start.4
  3.9 0.8 %copy-done.4 = bf16[2,48,144]{2,1,0:T(8,128)(2,1)S(1)} copy-done((bf16[2,48,144]{2,1,0:T(8,128)(2,1)S(1)}, bf16[2,48,144]{2,1,0:T(8,128)(2,1)}, u32[]{:S(2)}) %copy-start.4) | copy-done | bytes 27672
  4.7 0.0 copy-start.5
  4.7 0.8 %copy-done.5 = bf16[2,48,160]{2,1,0:T(8,128)(2,1)S(1)} copy-done((bf16[2,48,160]{2,1,0:T(8,128)(2,1)S(1)}, bf16[2,48,160]{2,1,0:T(8,128)(2,1)}, u32[]{:S(2)}) %copy-start.5) | copy-done | bytes 30744
  5.5 0.0 copy-start.6
  5.5 0.7 %copy-done.6 = f32[2]{0:T(128)S(1)} copy-done((f32[2]{0:T(128)S(1)}, f32[2]{0:T(128)}, u32[]{:S(2)}) %copy-start.6) | copy-done | bytes 32
  6.2 40.0 %shard_map.73 = f32[2,24,2304]{2,1,0:T(8,128)S(1)} custom-call(f32[2]{0:T(128)S(1)} %copy-done.6, f32[2,24,2304]{2,1,0:T(8,128)S(1)} %copy-done, f32[48,1152]{1,0:T(8,128)S(1)} %copy-done.3, f32[3,24,1152]{2,1,0:T(8,128)S(1)} %copy-done.2, bf16[2,48,160]{2,1,0:T(8,128)(2,1)S(1)} %copy-done.5, bf16[2,48,144]{2,1,0:T(8,128)(2,1)S(1)} %copy-done.4, ...), custom_call_target="tpu_custom_call" | custom-call | tf_op jit(solution)/shard_map/pallas_call | solution.py:271
  46.2 0.8 %copy.9 = f32[2,24,2304]{2,1,0:T(8,128)} copy(f32[2,24,2304]{2,1,0:T(8,128)S(1)} %shard_map.73) | data formatting | bytes 884736
Async XLA Ops:
  0.0 1.0 %copy-start = (f32[2,24,2304]{2,1,0:T(8,128)S(1)}, f32[2,24,2304]{2,1,0:T(8,128)}, u32[]{:S(2)}) copy-start(f32[2,24,2304]{2,1,0:T(8,128)} %psi_in.1) | copy-start | bytes 1327108
  1.0 1.0 %copy-start.1 = (f32[48,2304]{1,0:T(8,128)S(1)}, f32[48,2304]{1,0:T(8,128)}, u32[]{:S(2)}) copy-start(f32[48,2304]{1,0:T(8,128)} %constant.14.clone.coulomb_in) | copy-start | bytes 1327108
  2.0 1.0 %copy-start.2 = (f32[3,24,1152]{2,1,0:T(8,128)S(1)}, f32[3,24,1152]{2,1,0:T(8,128)}, u32[]{:S(2)}) copy-start(f32[3,24,1152]{2,1,0:T(8,128)} %constant.11.clone.y_in) | copy-start | bytes 995332
  3.0 0.9 %copy-start.3 = (f32[48,1152]{1,0:T(8,128)S(1)}, f32[48,1152]{1,0:T(8,128)}, u32[]{:S(2)}) copy-start(f32[48,1152]{1,0:T(8,128)} %constant.10.clone.z_in) | copy-start | bytes 663556
  3.9 0.8 %copy-start.4 = (bf16[2,48,144]{2,1,0:T(8,128)(2,1)S(1)}, bf16[2,48,144]{2,1,0:T(8,128)(2,1)}, u32[]{:S(2)}) copy-start(bf16[2,48,144]{2,1,0:T(8,128)(2,1)} %constant.13.clone.back_in) | copy-start | bytes 82948
  4.7 0.8 %copy-start.5 = (bf16[2,48,160]{2,1,0:T(8,128)(2,1)S(1)}, bf16[2,48,160]{2,1,0:T(8,128)(2,1)}, u32[]{:S(2)}) copy-start(bf16[2,48,160]{2,1,0:T(8,128)(2,1)} %constant.12.clone.there_in) | copy-start | bytes 92164
  5.5 0.7 %copy-start.6 = (f32[2]{0:T(128)S(1)}, f32[2]{0:T(128)}, u32[]{:S(2)}) copy-start(f32[2]{0:T(128)} %occ.1) | copy-start | bytes 28
